TPU v7x, 256 devices: a whole 4x4x8 slice. The times are simulated.
256 devices in a mesh: row: 16 (over z, x_hi), col: 8 (over y, core), mode: 2 (over x_lo).
Axes of the slice: x: 4 (x_hi: 2, x_lo: 2; x = x_hi * 2 + x_lo), y: 4, z: 8, core: 2. Of those that a mesh axis runs over, the one named last changes fastest.
Arguments:
- objects: float32 [2, 2, 4096, 2048], P(None, None, 'row', 'col'), may hold values from -4 to 4
- probes: float32 [2, 2, 128, 128], P('mode'), may hold values from -3 to 3
- phase: float32 [128, 128], replicated, may hold values from -3.140625 to 3.140625
- offsets: int32 [16, 8, 8, 2], P('row', 'col'), may hold values from 0 to 255
- measured: float32 [16, 8, 8, 128, 128], P('row', 'col'), may hold values from 0 to 2
Outputs:
- gradient: float32 [2, 2, 4096, 2048], P(None, None, 'row', 'col')
Inputs may be any that keep to these rules, and one draw needn't show every extreme that they name: `offsets`: windows start inside their own tile of 256 x 256 cells and reach up to 127 cells into the next tiles down and to the right.
All inputs are finite; a program needn't handle non-finite values.
Results may differ from a plain program's by a relative error of at most 0.0001.
Values sent between devices are 32-bit elements; how exact they have to be, the bound alone decides.
A program may use at most 64 MiB of HBM per device.

v0:
```python
import functools
import math

import jax
import jax.numpy as jnp
import numpy as np
from jax import lax
from jax.experimental import pallas as pl
from jax.experimental.pallas import tpu as pltpu
from jax.sharding import PartitionSpec as P

WIN = 128
LANES = 128
STEP = 2


def fourier_tables():
    counter = np.arange(WIN)
    angle = 2.0 * math.pi * (np.outer(counter, counter) % WIN) / WIN
    table_re, table_im = np.cos(angle) / math.sqrt(WIN), -np.sin(angle) / math.sqrt(WIN)
    forward = np.block([[table_re, table_im], [-table_im, table_re]])

    def parts(matrix):
        high = matrix.astype(jnp.bfloat16)
        return high, (matrix - high.astype(np.float64)).astype(jnp.bfloat16)

    f_high, f_low = parts(forward)
    i_high, i_low = parts(forward.T)
    right = np.stack([np.concatenate([f_high, f_high, f_low], 0), np.concatenate([i_high, i_high, i_low], 0)])
    left = np.stack([np.concatenate([i_high, i_high, i_low], 1), np.concatenate([f_high, f_high, f_low], 1)])
    return right, left


def halves(value):
    high = value.astype(jnp.bfloat16)
    return high, (value - high.astype(jnp.float32)).astype(jnp.bfloat16)


def along_rows(value, table):
    high, low = halves(value)
    return jnp.dot(jnp.concatenate([high, low, high], 1), table, preferred_element_type=jnp.float32)


def along_columns(value, table):
    high, low = halves(value)
    return jnp.dot(table, jnp.concatenate([high, low, high], 0), preferred_element_type=jnp.float32)


def beside_form(fields):
    return jnp.concatenate([jnp.concatenate(pair, 1) for pair in fields], 0)


def stacked_form(fields):
    return jnp.concatenate([jnp.concatenate(pair, 0) for pair in fields], 1)


def from_beside(value):
    return [
        (value[at : at + WIN, :WIN], value[at : at + WIN, WIN:])
        for at in range(0, value.shape[0], WIN)
    ]


def from_stacked(value):
    return [
        (value[:WIN, at : at + WIN], value[WIN:, at : at + WIN])
        for at in range(0, value.shape[1], WIN)
    ]


def forward_two(fields, right, left):
    rows_done = from_beside(along_rows(beside_form(fields), right[0]))
    return from_stacked(along_columns(stacked_form(rows_done), left[0]))


def inverse_two(fields, right, left):
    columns_done = from_stacked(along_columns(stacked_form(fields), left[1]))
    return from_beside(along_rows(beside_form(columns_done), right[1]))


def times(a, b):
    return a[0] * b[0] - a[1] * b[1], a[0] * b[1] + a[1] * b[0]


def times_conj(a, b):
    return a[0] * b[0] + a[1] * b[1], a[1] * b[0] - a[0] * b[1]


def kernel(
    offsets, objects, probes, phase, measured, rim_right, rim_low, right, left,
    own_out, right_out, low_out,
    ext, middle, prop, spread, total, target, sems,
):
    count = measured.shape[0]
    copies = []

    def fetch(src, dst):
        copy = pltpu.make_async_copy(src, dst, sems.at[len(copies)])
        copy.start()
        copies.append(copy)

    for s in range(2):
        for j in range(2):
            fetch(objects.at[s, :, :, pl.ds(LANES * j, LANES)], ext.at[s, :, j, pl.ds(0, 256), :])
        fetch(rim_right.at[s], ext.at[s, :, 2, pl.ds(0, 256), :])
        for j in range(3):
            fetch(rim_low.at[s, :, :, pl.ds(LANES * j, LANES)], ext.at[s, :, j, pl.ds(256, WIN), :])
    fetch(measured, target)

    spread[...] = jnp.zeros_like(spread)
    prop[0] = jnp.cos(phase[...])
    prop[1] = jnp.sin(phase[...])
    for copy in copies:
        copy.wait()

    lane = lax.broadcasted_iota(jnp.int32, (WIN, LANES), 1)

    def window(s, p):
        r0, c0 = offsets[p, 0], offsets[p, 1]
        tile = c0 // LANES
        shift = c0 % LANES
        back = (LANES - shift) % LANES

        def part(c):
            first = pltpu.roll(ext[s, c, tile, pl.ds(r0, WIN), :], back, 1)
            second = pltpu.roll(ext[s, c, tile + 1, pl.ds(r0, WIN), :], back, 1)
            return jnp.where(lane < LANES - shift, first, second)

        return part(0), part(1)

    def leave(p, patch):
        shift = offsets[p, 1] % LANES
        for c in range(2):
            rolled = pltpu.roll(patch[c], shift, 1)
            spread[4 * p + 2 * c, pl.ds(256, WIN), :] = jnp.where(lane >= shift, rolled, 0.0)
            spread[4 * p + 2 * c + 1, pl.ds(256, WIN), :] = jnp.where(lane < shift, rolled, 0.0)

    def gather(s):
        for c in range(2):
            for j in range(3):
                def block(at, _, c=c, j=j):
                    row = at * WIN
                    value = jnp.zeros((WIN, LANES), jnp.float32)
                    for p in range(count):
                        r0, tile = offsets[p, 0], offsets[p, 1] // LANES
                        index = jnp.where(
                            tile == j, 4 * p + 2 * c, jnp.where(tile == j - 1, 4 * p + 2 * c + 1, 4 * count)
                        )
                        value += spread[index, pl.ds(256 - r0 + row, WIN), :]
                    total[s, c, j, pl.ds(pl.multiple_of(row, WIN), WIN), :] = value
                    return 0

                lax.fori_loop(0, 3, block, 0)

    modes = [(probes[m, 0], probes[m, 1]) for m in range(2)]
    passage = (prop[0], prop[1])

    def first_phase(step, _):
        for k in range(STEP):
            p = step * STEP + k
            view = window(0, p)
            spectrum = forward_two([times(mode, view) for mode in modes], right, left)
            field = inverse_two([times(passage, one) for one in spectrum], right, left)
            middle[p] = beside_form(field)
        return 0

    def second_phase(step, _):
        for k in range(STEP):
            p = step * STEP + k
            view = window(1, p)
            field = from_beside(middle[p])
            far = forward_two([times(one, view) for one in field], right, left)
            power = sum(one[0] * one[0] + one[1] * one[1] for one in far)
            weight = 4.0 * (power - target[p])
            gexit = inverse_two([(weight * one[0], weight * one[1]) for one in far], right, left)
            pieces = [times_conj(g, b) for g, b in zip(gexit, field)]
            leave(p, (pieces[0][0] + pieces[1][0], pieces[0][1] + pieces[1][1]))
            middle[p] = beside_form([times_conj(g, view) for g in gexit])
        return 0

    def third_phase(step, _):
        for k in range(STEP):
            p = step * STEP + k
            spectrum = forward_two(from_beside(middle[p]), right, left)
            wave = inverse_two([times_conj(one, passage) for one in spectrum], right, left)
            pieces = [times_conj(g, mode) for g, mode in zip(wave, modes)]
            leave(p, (pieces[0][0] + pieces[1][0], pieces[0][1] + pieces[1][1]))
        return 0

    lax.fori_loop(0, count // STEP, first_phase, 0)
    lax.fori_loop(0, count // STEP, second_phase, 0)
    gather(1)
    lax.fori_loop(0, count // STEP, third_phase, 0)
    gather(0)

    copies.clear()
    for s in range(2):
        for j in range(2):
            fetch(total.at[s, :, j, pl.ds(0, 256), :], own_out.at[s, :, :, pl.ds(LANES * j, LANES)])
        fetch(total.at[s, :, 2, pl.ds(0, 256), :], right_out.at[s])
        for j in range(3):
            fetch(total.at[s, :, j, pl.ds(256, WIN), :], low_out.at[s, :, :, pl.ds(LANES * j, LANES)])
    for copy in copies:
        copy.wait()


def tile_gradient(offsets, objects, probes, phase, measured, rim_right, rim_low):
    right, left = fourier_tables()
    count = measured.shape[0]
    anywhere = pl.BlockSpec(memory_space=pl.ANY)
    whole = pl.BlockSpec(memory_space=pltpu.VMEM)
    shape = jax.ShapeDtypeStruct
    return pl.pallas_call(
        kernel,
        out_shape=(
            shape((2, 2, 256, 256), jnp.float32),
            shape((2, 2, 256, WIN), jnp.float32),
            shape((2, 2, WIN, 384), jnp.float32),
        ),
        in_specs=[
            pl.BlockSpec(memory_space=pltpu.SMEM), anywhere, whole, whole, anywhere, anywhere, anywhere, whole, whole,
        ],
        out_specs=(anywhere, anywhere, anywhere),
        scratch_shapes=[
            pltpu.VMEM((2, 2, 3, 384, LANES), jnp.float32),
            pltpu.VMEM((count, 256, 256), jnp.float32),
            pltpu.VMEM((2, WIN, WIN), jnp.float32),
            pltpu.VMEM((4 * count + 1, 640, LANES), jnp.float32),
            pltpu.VMEM((2, 2, 3, 384, LANES), jnp.float32),
            pltpu.VMEM((count, WIN, WIN), jnp.float32),
            pltpu.SemaphoreType.DMA((16,)),
        ],
        compiler_params=pltpu.CompilerParams(vmem_limit_bytes=60 * 2**20),
        name="tile_gradient",
    )(offsets, objects, probes, phase, measured, rim_right, rim_low, jnp.asarray(right), jnp.asarray(left))


def on_device(objects, probes, phase, offsets, measured):
    rows, cols = lax.axis_size("row"), lax.axis_size("col")
    tile_len = objects.shape[2]
    leftward = [(i, i - 1) for i in range(1, cols)]
    rightward = [(j, i) for i, j in leftward]
    upward = [(2 * i + m, 2 * (i - 1) + 1 - m) for i in range(1, rows) for m in range(2)]
    downward = [(j, i) for i, j in upward]

    other = lax.ppermute(probes, "mode", [(0, 1), (1, 0)])
    is_first = lax.axis_index("mode") == 0
    both = jnp.concatenate([jnp.where(is_first, probes, other), jnp.where(is_first, other, probes)], 0)
    rim_right = lax.ppermute(objects[:, :, :, :WIN], "col", leftward)
    top = jnp.concatenate([objects[:, :, :WIN], rim_right[:, :, :WIN]], 3)
    rim_low = lax.ppermute(top, ("row", "mode"), upward)

    own, beside, below = tile_gradient(offsets[0, 0], objects, both, phase, measured[0, 0], rim_right, rim_low)

    fallen = lax.ppermute(below, ("row", "mode"), downward)
    beside = beside.at[:, :, :WIN].add(fallen[:, :, :, tile_len:])
    moved = lax.ppermute(beside, "col", rightward)
    own = own.at[:, :, :WIN].add(fallen[:, :, :, :tile_len])
    return own.at[:, :, :, :WIN].add(moved)


def solution(mesh):
    placed = (
        P(None, None, "row", "col"),
        P("mode", None, None, None),
        P(),
        P("row", "col", None, None),
        P("row", "col", None, None, None),
    )
    return jax.shard_map(
        on_device,
        mesh=mesh,
        in_specs=placed,
        out_specs=P(None, None, "row", "col"),
        check_vma=False,
    )
```

profile of v0, /device:TPU:110, one launch (start us, length us, event | category | flops | bytes accessed | tf_op | source)
XLA Modules:
  0.0 109.4 jit_solution(15779081186433583996)
XLA Ops:
  0.0 1.1 slice.102
  1.1 0.0 slice-start
  1.1 2.1 %collective-permute-start.1 = (f32[2,2,256,128]{3,2,1,0:T(8,128)S(1)}, f32[2,2,256,128]{3,2,1,0:T(8,128)S(1)}, u32[]{:S(2)}, u32[]{:S(2)}) collective-permute-start(f32[2,2,256,128]{3,2,1,0:T(8,128)S(1)} %slice.102), channel_id=1, source_target_pairs={{2,0},{4,2},{6,4},{8,6},{10,8},{12,10},{14,12},{3,1},{5,3},{7,5},{... | collective-permute-start | bytes 1572872 | tf_op jit(solution)/shard_map/ppermute | solution.py:249
  3.2 6.7 %collective-permute-done.1.rim_right = f32[2,2,256,128]{3,2,1,0:T(8,128)S(1)} collective-permute-done((f32[2,2,256,128]{3,2,1,0:T(8,128)S(1)}, f32[2,2,256,128]{3,2,1,0:T(8,128)S(1)}, u32[]{:S(2)}, u32[]{:S(2)}) %collective-permute-start.1) | collective-permute-done | bytes 524320 | tf_op jit(solution)/shard_map/ppermute | solution.py:249
  9.8 0.0 copy-start
  9.9 0.0 slice-done
  9.9 0.0 copy-start.2
  9.9 0.1 pad_maximum_fusion
  9.9 0.7 copy-done
  10.6 2.4 %collective-permute-start.2 = (f32[2,2,128,384]{3,2,1,0:T(8,128)S(1)}, f32[2,2,128,384]{3,2,1,0:T(8,128)S(1)}, u32[]{:S(2)}, u32[]{:S(2)}) collective-permute-start(f32[2,2,128,384]{3,2,1,0:T(8,128)S(1)} %pad_maximum_fusion), channel_id=1, source_target_pairs={{16,1},{17,0},{32,17},{33,16},{48,33},{49,32},{64,49},{65,48},{80,... | collective-permute-start | bytes 2359304 | tf_op jit(solution)/shard_map/ppermute | solution.py:251
  13.0 0.0 copy-done.2
  13.0 1.0 collective-permute-start
  14.0 0.0 copy-start.3
  14.0 0.7 copy-done.3
  14.7 0.7 copy.8.offsets
  15.4 3.5 %collective-permute-done = f32[1,2,128,128]{3,2,1,0:T(8,128)S(1)} collective-permute-done((f32[1,2,128,128]{3,2,1,0:T(8,128)S(1)}, f32[1,2,128,128]{3,2,1,0:T(8,128)S(1)}, u32[]{:S(2)}, u32[]{:S(2)}) %collective-permute-start) | collective-permute-done | bytes 131104 | tf_op jit(solution)/shard_map/ppermute | solution.py:246
  18.9 0.7 pad_maximum_fusion.1.probes
  19.6 15.7 %collective-permute-done.2.rim_low = f32[2,2,128,384]{3,2,1,0:T(8,128)S(1)} collective-permute-done((f32[2,2,128,384]{3,2,1,0:T(8,128)S(1)}, f32[2,2,128,384]{3,2,1,0:T(8,128)S(1)}, u32[]{:S(2)}, u32[]{:S(2)}) %collective-permute-start.2) | collective-permute-done | bytes 786464 | tf_op jit(solution)/shard_map/ppermute | solution.py:251
  35.4 0.0 copy-start.1
  35.4 0.9 copy-done.1
  36.3 35.3 %tile_gradient.1 = (f32[2,2,256,256]{3,2,1,0:T(8,128)}, f32[2,2,256,128]{3,2,1,0:T(8,128)}, f32[2,2,128,384]{3,2,1,0:T(8,128)}) custom-call(s32[8,2]{1,0:T(8,128)} %copy.8.offsets, f32[2,2,256,256]{3,2,1,0:T(8,128)} %objects.1, f32[2,2,128,128]{3,2,1,0:T(8,128)} %pad_maximum_fusion.1.probes, f32[128,128]{1,0:T(8,128)} %phase.1, f32[8,128,128]{2,1,0:T(8,128)} %bitcast.2, ...), custom_call_target="tpu_custom_call" | custom-call | tf_op jit(solution)/shard_map/tile_gradient/pallas_call | solution.py:213
  71.6 2.8 %collective-permute-start.3 = (f32[2,2,128,384]{3,2,1,0:T(8,128)}, f32[2,2,128,384]{3,2,1,0:T(8,128)S(1)}, u32[]{:S(2)}, u32[]{:S(2)}) collective-permute-start(f32[2,2,128,384]{3,2,1,0:T(8,128)} %get-tuple-element.45), channel_id=1, source_target_pairs={{1,16},{0,17},{17,32},{16,33},{33,48},{32,49},{49,64},{48,65},{65,... | collective-permute-start | bytes 2359304 | tf_op jit(solution)/shard_map/ppermute | solution.py:255
  74.4 20.6 %collective-permute-done.3 = f32[2,2,128,384]{3,2,1,0:T(8,128)S(1)} collective-permute-done((f32[2,2,128,384]{3,2,1,0:T(8,128)}, f32[2,2,128,384]{3,2,1,0:T(8,128)S(1)}, u32[]{:S(2)}, u32[]{:S(2)}) %collective-permute-start.3) | collective-permute-done | bytes 786464 | tf_op jit(solution)/shard_map/ppermute | solution.py:255
  95.1 1.7 %fusion.2 = f32[2,2,256,128]{3,2,1,0:T(8,128)} fusion(f32[2,2,256,128]{3,2,1,0:T(8,128)} %get-tuple-element.46, f32[2,2,128,384]{3,2,1,0:T(8,128)S(1)} %collective-permute-done.3), kind=kLoop, calls=%fused_computation.6 | loop fusion | flops 65536 | bytes 786432 | tf_op jit(solution)/shard_map/scatter-add | solution.py:256
  96.8 1.9 %collective-permute-start.4 = (f32[2,2,256,128]{3,2,1,0:T(8,128)}, f32[2,2,256,128]{3,2,1,0:T(8,128)S(1)}, u32[]{:S(2)}, u32[]{:S(2)}) collective-permute-start(f32[2,2,256,128]{3,2,1,0:T(8,128)} %fusion.2), channel_id=1, source_target_pairs={{0,2},{2,4},{4,6},{6,8},{8,10},{10,12},{12,14},{1,3},{3,5},{5,7},{... | collective-permute-start | bytes 1572872 | tf_op jit(solution)/shard_map/ppermute | solution.py:257
  98.7 1.9 %fusion.1 = f32[2,2,256,256]{3,2,1,0:T(8,128)} fusion(f32[2,2,256,256]{3,2,1,0:T(8,128)} %get-tuple-element.44, f32[2,2,128,384]{3,2,1,0:T(8,128)S(1)} %collective-permute-done.3), kind=kLoop, calls=%fused_computation.4 | loop fusion | flops 131072 | bytes 1572864 | tf_op jit(solution)/shard_map/scatter-add | solution.py:258
  100.6 6.9 %collective-permute-done.4 = f32[2,2,256,128]{3,2,1,0:T(8,128)S(1)} collective-permute-done((f32[2,2,256,128]{3,2,1,0:T(8,128)}, f32[2,2,256,128]{3,2,1,0:T(8,128)S(1)}, u32[]{:S(2)}, u32[]{:S(2)}) %collective-permute-start.4) | collective-permute-done | bytes 524320 | tf_op jit(solution)/shard_map/ppermute | solution.py:257
  107.5 1.9 %fusion = f32[2,2,256,256]{3,2,1,0:T(8,128)} fusion(f32[2,2,256,256]{3,2,1,0:T(8,128)} %fusion.1, f32[2,2,256,128]{3,2,1,0:T(8,128)S(1)} %collective-permute-done.4), kind=kLoop, calls=%fused_computation.2 | loop fusion | flops 131072 | bytes 1572864 | tf_op jit(solution)/shard_map/scatter-add | solution.py:259
  (2 shorter events, 0.0 us)
Async XLA Ops:
  1.1 8.8 %slice-start = ((f32[2,2,256,256]{3,2,1,0:T(8,128)}), f32[2,2,128,256]{3,2,1,0:T(8,128)S(1)}, s32[]{:S(2)}) async-start(f32[2,2,256,256]{3,2,1,0:T(8,128)} %objects.1), calls=%async_computation | async-start | bytes 1048576 | tf_op jit(solution)/shard_map/slice | solution.py:250
  1.1 8.7 %collective-permute-start.1 = (f32[2,2,256,128]{3,2,1,0:T(8,128)S(1)}, f32[2,2,256,128]{3,2,1,0:T(8,128)S(1)}, u32[]{:S(2)}, u32[]{:S(2)}) collective-permute-start(f32[2,2,256,128]{3,2,1,0:T(8,128)S(1)} %slice.102), channel_id=1, source_target_pairs={{2,0},{4,2},{6,4},{8,6},{10,8},{12,10},{14,12},{3,1},{5,3},{7,5},{... | collective-permute-start | bytes 1572872 | tf_op jit(solution)/shard_map/ppermute | solution.py:249
  9.8 0.8 copy-start
  9.9 3.2 %copy-start.2 = (f32[1,2,128,128]{3,2,1,0:T(8,128)S(1)}, f32[1,2,128,128]{3,2,1,0:T(8,128)}, u32[]{:S(2)}) copy-start(f32[1,2,128,128]{3,2,1,0:T(8,128)} %param.14) | copy-start | bytes 393220
  10.6 24.7 %collective-permute-start.2 = (f32[2,2,128,384]{3,2,1,0:T(8,128)S(1)}, f32[2,2,128,384]{3,2,1,0:T(8,128)S(1)}, u32[]{:S(2)}, u32[]{:S(2)}) collective-permute-start(f32[2,2,128,384]{3,2,1,0:T(8,128)S(1)} %pad_maximum_fusion), channel_id=1, source_target_pairs={{16,1},{17,0},{32,17},{33,16},{48,33},{49,32},{64,49},{65,48},{80,... | collective-permute-start | bytes 2359304 | tf_op jit(solution)/shard_map/ppermute | solution.py:251
  13.0 5.9 %collective-permute-start = (f32[1,2,128,128]{3,2,1,0:T(8,128)S(1)}, f32[1,2,128,128]{3,2,1,0:T(8,128)S(1)}, u32[]{:S(2)}, u32[]{:S(2)}) collective-permute-start(f32[1,2,128,128]{3,2,1,0:T(8,128)S(1)} %copy-done.2), channel_id=1, source_target_pairs={{0,1},{1,0},{2,3},{3,2},{4,5},{5,4},{6,7},{7,6},{8,9},{9,8},{10,11... | collective-permute-start | bytes 393224 | tf_op jit(solution)/shard_map/ppermute | solution.py:246
  14.0 0.7 copy-start.3
  35.4 0.9 copy-start.1
  71.6 23.5 %collective-permute-start.3 = (f32[2,2,128,384]{3,2,1,0:T(8,128)}, f32[2,2,128,384]{3,2,1,0:T(8,128)S(1)}, u32[]{:S(2)}, u32[]{:S(2)}) collective-permute-start(f32[2,2,128,384]{3,2,1,0:T(8,128)} %get-tuple-element.45), channel_id=1, source_target_pairs={{1,16},{0,17},{17,32},{16,33},{33,48},{32,49},{49,64},{48,65},{65,... | collective-permute-start | bytes 2359304 | tf_op jit(solution)/shard_map/ppermute | solution.py:255
  96.8 10.7 %collective-permute-start.4 = (f32[2,2,256,128]{3,2,1,0:T(8,128)}, f32[2,2,256,128]{3,2,1,0:T(8,128)S(1)}, u32[]{:S(2)}, u32[]{:S(2)}) collective-permute-start(f32[2,2,256,128]{3,2,1,0:T(8,128)} %fusion.2), channel_id=1, source_target_pairs={{0,2},{2,4},{4,6},{6,8},{8,10},{10,12},{12,14},{1,3},{3,5},{5,7},{... | collective-permute-start | bytes 1572872 | tf_op jit(solution)/shard_map/ppermute | solution.py:257
where the time goes:
time: 110 us; the launch traced here: 109 us
  waiting for transfers between devices  53.5 us (49%)
  Pallas kernels  35.3 us (32%)
  starting transfers between devices  10.1 us (9%)
  other arithmetic  6.34 us (6%)
  local copies, waits for them, and re-layouts  4.04 us (4%)
    pallas_call x1, Pallas kernels, tile_gradient(): pl.pallas_call(kernel, out_shape=(shape((2, 2, 256, 256), jnp.float32), s...  35.3 us
    ppermute x1, waiting for transfers between devices, on_device(): fallen = lax.ppermute(below, ('row', 'mode'), downward)  20.6 us
    ppermute x1, waiting for transfers between devices, on_device(): rim_low = lax.ppermute(top, ('row', 'mode'), upward)  15.7 us
    ppermute x1, waiting for transfers between devices, on_device(): moved = lax.ppermute(beside, 'col', rightward)  6.87 us
    ppermute x1, waiting for transfers between devices, on_device(): rim_right = lax.ppermute(objects[:, :, :, :WIN], 'col', leftward)  6.68 us
    ppermute x1, waiting for transfers between devices, on_device(): other = lax.ppermute(probes, 'mode', [(0, 1), (1, 0)])  3.53 us
    ppermute x1, starting transfers between devices, on_device(): fallen = lax.ppermute(below, ('row', 'mode'), downward)  2.83 us
    ppermute x1, starting transfers between devices, on_device(): rim_low = lax.ppermute(top, ('row', 'mode'), upward)  2.37 us
  transfers between devices with their start and end apart: 5, of which 5 were waited for; matrix products, arithmetic and copies ran while one was open for 3% of the time, Pallas kernels for 0%

commit v1 on v0

v1 whole, which is shorter than its diff:
```python
import functools
import math

import jax
import jax.numpy as jnp
import numpy as np
from jax import lax
from jax.experimental import pallas as pl
from jax.experimental.pallas import tpu as pltpu
from jax.sharding import PartitionSpec as P

WIN = 128
LANES = 128
STEP = 2
MESH = pl.DeviceIdType.MESH


def fourier_tables():
    counter = np.arange(WIN)
    angle = 2.0 * math.pi * (np.outer(counter, counter) % WIN) / WIN
    table_re, table_im = np.cos(angle) / math.sqrt(WIN), -np.sin(angle) / math.sqrt(WIN)
    forward = np.block([[table_re, table_im], [-table_im, table_re]])

    def parts(matrix):
        high = matrix.astype(jnp.bfloat16)
        return high, (matrix - high.astype(np.float64)).astype(jnp.bfloat16)

    f_high, f_low = parts(forward)
    i_high, i_low = parts(forward.T)
    right = np.stack([np.concatenate([f_high, f_high, f_low], 0), np.concatenate([i_high, i_high, i_low], 0)])
    left = np.stack([np.concatenate([i_high, i_high, i_low], 1), np.concatenate([f_high, f_high, f_low], 1)])
    return right, left


def halves(value):
    high = value.astype(jnp.bfloat16)
    return high, (value - high.astype(jnp.float32)).astype(jnp.bfloat16)


def along_rows(value, table):
    high, low = halves(value)
    return jnp.dot(jnp.concatenate([high, low, high], 1), table, preferred_element_type=jnp.float32)


def along_columns(value, table):
    high, low = halves(value)
    return jnp.dot(table, jnp.concatenate([high, low, high], 0), preferred_element_type=jnp.float32)


def beside_form(fields):
    return jnp.concatenate([jnp.concatenate(pair, 1) for pair in fields], 0)


def stacked_form(fields):
    return jnp.concatenate([jnp.concatenate(pair, 0) for pair in fields], 1)


def from_beside(value):
    return [
        (value[at : at + WIN, :WIN], value[at : at + WIN, WIN:])
        for at in range(0, value.shape[0], WIN)
    ]


def from_stacked(value):
    return [
        (value[:WIN, at : at + WIN], value[WIN:, at : at + WIN])
        for at in range(0, value.shape[1], WIN)
    ]


def forward_two(fields, right, left):
    rows_done = from_beside(along_rows(beside_form(fields), right[0]))
    return from_stacked(along_columns(stacked_form(rows_done), left[0]))


def inverse_two(fields, right, left):
    columns_done = from_stacked(along_columns(stacked_form(fields), left[1]))
    return from_beside(along_rows(beside_form(columns_done), right[1]))


def times(a, b):
    return a[0] * b[0] - a[1] * b[1], a[0] * b[1] + a[1] * b[0]


def times_conj(a, b):
    return a[0] * b[0] + a[1] * b[1], a[1] * b[0] - a[0] * b[1]


def kernel(
    offsets, objects, probes, phase, measured, right_in, left_in,
    out,
    ext_first, ext_second, both, middle, angle, prop, spread, total, fallen, moved, target, right, left,
    sems, send, recv,
):
    rows, cols = lax.axis_size("row"), lax.axis_size("col")
    row, col, mode = lax.axis_index("row"), lax.axis_index("col"), lax.axis_index("mode")
    other = 1 - mode
    has_up, has_left, has_down, has_right = row > 0, col > 0, row < rows - 1, col < cols - 1
    count = target.shape[0]

    def device(d_row, d_col, which):
        return {"row": (row + d_row + rows) % rows, "col": (col + d_col + cols) % cols, "mode": which}

    up, down = device(-1, 0, other), device(1, 0, other)
    leftward, rightward = device(0, -1, mode), device(0, 1, mode)
    up_left, down_right = device(-1, -1, other), device(1, 1, other)
    partner = device(0, 0, other)

    def fetch(src, dst, k):
        return pltpu.make_async_copy(src, dst, sems.at[k])

    def remote(src, dst, k, to):
        return pltpu.make_async_remote_copy(
            src_ref=src, dst_ref=dst, send_sem=send.at[k], recv_sem=recv.at[k], device_id=to, device_id_type=MESH
        )

    below, beside = pl.ds(256, WIN), pl.ds(0, 256)
    ext = (ext_first, ext_second)

    own = [
        [fetch(objects.at[s, :, :, pl.ds(LANES * j, LANES)], ext[s].at[:, j, beside, :], 2 * s + j) for j in range(2)]
        for s in range(2)
    ]
    needed = [
        fetch(probes.at[0], both.at[mode], 4),
        fetch(right_in, right, 5),
        fetch(left_in, left, 6),
    ]
    get_phase = fetch(phase, angle, 7)
    get_target = fetch(measured.at[0, 0], target, 8)
    for copy in [get_phase, *own[0], *needed, *own[1], get_target]:
        copy.start()

    barrier = pltpu.get_barrier_semaphore()
    everyone = (up, down, leftward, rightward, up_left, down_right, partner)
    for one in everyone:
        pl.semaphore_signal(barrier, inc=1, device_id=one, device_id_type=MESH)
    pl.semaphore_wait(barrier, len(everyone))

    def in_low(s, j, which):
        return remote(
            objects.at[s, which, pl.ds(0, WIN), pl.ds(LANES * j, LANES)], ext[s].at[which, j, below, :], 8 * s + j, up
        )

    def in_corner(s, which):
        return remote(
            objects.at[s, which, pl.ds(0, WIN), pl.ds(0, LANES)], ext[s].at[which, 2, below, :], 8 * s + 2, up_left
        )

    def in_right(s, c):
        return remote(objects.at[s, c, :, pl.ds(0, LANES)], ext[s].at[c, 2, beside, :], 8 * s + 3 + c, leftward)

    def in_pass(s, j, which):
        return remote(ext[s].at[which, j, below, :], ext[s].at[which, j, below, :], 8 * s + 5 + j, partner)

    share = remote(probes.at[0], both.at[mode], 32, partner)

    def out_low(s, j, which):
        return remote(total.at[s, which, j, below, :], fallen.at[s, which, j], 16 + 8 * s + j, down)

    def out_corner(s, which):
        return remote(total.at[s, which, 2, below, :], fallen.at[s, which, 2], 16 + 8 * s + 2, down_right)

    def out_right(s, c):
        return remote(total.at[s, c, 2, beside, :], moved.at[s, c], 16 + 8 * s + 3 + c, rightward)

    def out_pass(s, j, which):
        return remote(fallen.at[s, which, j], fallen.at[s, which, j], 16 + 8 * s + 5 + j, partner)

    for s in range(2):
        @pl.when(has_up)
        def _(s=s):
            for j in range(2):
                in_low(s, j, other).start()

        @pl.when(has_left)
        def _(s=s):
            for c in range(2):
                in_right(s, c).start()

        @pl.when(has_up & has_left)
        def _(s=s):
            in_corner(s, other).start()

        if s == 0:
            share.start()

    @pl.when(jnp.logical_not(has_down))
    def _():
        for s in range(2):
            for c in range(2):
                for j in range(3):
                    ext[s][c, j, below, :] = jnp.zeros((WIN, LANES), jnp.float32)

    @pl.when(jnp.logical_not(has_right))
    def _():
        for s in range(2):
            for c in range(2):
                ext[s][c, 2, beside, :] = jnp.zeros((256, LANES), jnp.float32)

    @pl.when(has_down & jnp.logical_not(has_right))
    def _():
        for s in range(2):
            for c in range(2):
                ext[s][c, 2, below, :] = jnp.zeros((WIN, LANES), jnp.float32)

    spread[...] = jnp.zeros_like(spread)
    get_phase.wait()
    prop[0] = jnp.cos(angle[...])
    prop[1] = jnp.sin(angle[...])

    def hand_in(s, j):
        if j < 2:
            @pl.when(has_down)
            def _():
                in_low(s, j, mode).wait_recv()
                in_pass(s, j, mode).start()
        else:
            @pl.when(has_down & has_right)
            def _():
                in_corner(s, mode).wait_recv()
                in_pass(s, j, mode).start()

    def arrive_in(s):
        for copy in own[s]:
            copy.wait()

        @pl.when(has_right)
        def _():
            for c in range(2):
                in_right(s, c).wait_recv()

        @pl.when(has_down)
        def _():
            for j in range(2):
                in_pass(s, j, other).wait_recv()

        @pl.when(has_down & has_right)
        def _():
            in_pass(s, 2, other).wait_recv()

    def send_out(s):
        @pl.when(has_down)
        def _():
            for j in range(2):
                out_low(s, j, other).start()

        @pl.when(has_right)
        def _():
            for c in range(2):
                out_right(s, c).start()

        @pl.when(has_down & has_right)
        def _():
            out_corner(s, other).start()

    def hand_out(s, j):
        if j < 2:
            @pl.when(has_up)
            def _():
                out_low(s, j, mode).wait_recv()
                out_pass(s, j, mode).start()
        else:
            @pl.when(has_up & has_left)
            def _():
                out_corner(s, mode).wait_recv()
                out_pass(s, j, mode).start()

    def arrive_out(s):
        @pl.when(has_left)
        def _():
            for c in range(2):
                out_right(s, c).wait_recv()
                total[s, c, 0, beside, :] += moved[s, c]

        @pl.when(has_up)
        def _():
            for j in range(2):
                out_pass(s, j, other).wait_recv()
                for c in range(2):
                    total[s, c, j, pl.ds(0, WIN), :] += fallen[s, c, j]

        @pl.when(has_up & has_left)
        def _():
            out_pass(s, 2, other).wait_recv()
            for c in range(2):
                total[s, c, 0, pl.ds(0, WIN), :] += fallen[s, c, 2]

    def result(s):
        return [
            fetch(total.at[s, :, j, beside, :], out.at[s, :, :, pl.ds(LANES * j, LANES)], 9 + 2 * s + j)
            for j in range(2)
        ]

    lane = lax.broadcasted_iota(jnp.int32, (WIN, LANES), 1)

    def window(s, p):
        r0, c0 = offsets[0, 0, p, 0], offsets[0, 0, p, 1]
        tile = c0 // LANES
        shift = c0 % LANES
        back = (LANES - shift) % LANES

        def part(c):
            first = pltpu.roll(ext[s][c, tile, pl.ds(r0, WIN), :], back, 1)
            second = pltpu.roll(ext[s][c, tile + 1, pl.ds(r0, WIN), :], back, 1)
            return jnp.where(lane < LANES - shift, first, second)

        return part(0), part(1)

    def leave(p, patch):
        shift = offsets[0, 0, p, 1] % LANES
        for c in range(2):
            rolled = pltpu.roll(patch[c], shift, 1)
            spread[4 * p + 2 * c, pl.ds(256, WIN), :] = jnp.where(lane >= shift, rolled, 0.0)
            spread[4 * p + 2 * c + 1, pl.ds(256, WIN), :] = jnp.where(lane < shift, rolled, 0.0)

    def gather(s, blocks):
        for c in range(2):
            for j, at in blocks:
                value = jnp.zeros((WIN, LANES), jnp.float32)
                for p in range(count):
                    r0, tile = offsets[0, 0, p, 0], offsets[0, 0, p, 1] // LANES
                    index = jnp.where(
                        tile == j, 4 * p + 2 * c, jnp.where(tile == j - 1, 4 * p + 2 * c + 1, 4 * count)
                    )
                    value += spread[index, pl.ds(256 - r0 + WIN * at, WIN), :]
                total[s, c, j, pl.ds(WIN * at, WIN), :] = value

    rims = [(0, 2), (1, 2), (2, 2), (2, 0), (2, 1)]
    inside = [(0, 0), (0, 1), (1, 0), (1, 1)]

    for j in range(3):
        hand_in(0, j)
    for copy in needed:
        copy.wait()
    share.wait_recv()
    arrive_in(0)

    modes = [(both[m, 0], both[m, 1]) for m in range(2)]
    passage = (prop[0], prop[1])

    def first_phase(step, _):
        for j in range(3):
            @pl.when(step == j + 1)
            def _(j=j):
                hand_in(1, j)

        for k in range(STEP):
            p = step * STEP + k
            view = window(0, p)
            spectrum = forward_two([times(mode, view) for mode in modes], right, left)
            field = inverse_two([times(passage, one) for one in spectrum], right, left)
            middle[p] = beside_form(field)
        return 0

    def second_phase(step, _):
        for k in range(STEP):
            p = step * STEP + k
            view = window(1, p)
            field = from_beside(middle[p])
            far = forward_two([times(one, view) for one in field], right, left)
            power = sum(one[0] * one[0] + one[1] * one[1] for one in far)
            weight = 4.0 * (power - target[p])
            gexit = inverse_two([(weight * one[0], weight * one[1]) for one in far], right, left)
            pieces = [times_conj(g, b) for g, b in zip(gexit, field)]
            leave(p, (pieces[0][0] + pieces[1][0], pieces[0][1] + pieces[1][1]))
            middle[p] = beside_form([times_conj(g, view) for g in gexit])
        return 0

    def third_phase(step, _):
        for j in range(3):
            @pl.when(step == j + 1)
            def _(j=j):
                hand_out(1, j)

        for k in range(STEP):
            p = step * STEP + k
            spectrum = forward_two(from_beside(middle[p]), right, left)
            wave = inverse_two([times_conj(one, passage) for one in spectrum], right, left)
            pieces = [times_conj(g, mode) for g, mode in zip(wave, modes)]
            leave(p, (pieces[0][0] + pieces[1][0], pieces[0][1] + pieces[1][1]))
        return 0

    lax.fori_loop(0, count // STEP, first_phase, 0)
    arrive_in(1)
    get_target.wait()
    lax.fori_loop(0, count // STEP, second_phase, 0)
    gather(1, rims)
    send_out(1)
    gather(1, inside)
    lax.fori_loop(0, count // STEP, third_phase, 0)
    gather(0, rims)
    send_out(0)
    gather(0, inside)
    arrive_out(1)
    for copy in result(1):
        copy.start()
    for j in range(3):
        hand_out(0, j)
    arrive_out(0)
    for copy in result(0):
        copy.start()

    share.wait_send()
    for s in range(2):
        @pl.when(has_up)
        def _(s=s):
            for j in range(2):
                in_low(s, j, other).wait_send()
                out_pass(s, j, mode).wait_send()

        @pl.when(has_left)
        def _(s=s):
            for c in range(2):
                in_right(s, c).wait_send()

        @pl.when(has_up & has_left)
        def _(s=s):
            in_corner(s, other).wait_send()
            out_pass(s, 2, mode).wait_send()

        @pl.when(has_down)
        def _(s=s):
            for j in range(2):
                in_pass(s, j, mode).wait_send()
                out_low(s, j, other).wait_send()

        @pl.when(has_right)
        def _(s=s):
            for c in range(2):
                out_right(s, c).wait_send()

        @pl.when(has_down & has_right)
        def _(s=s):
            in_pass(s, 2, mode).wait_send()
            out_corner(s, other).wait_send()

        for copy in result(s):
            copy.wait()


def on_device(objects, probes, phase, offsets, measured):
    right, left = fourier_tables()
    count = measured.shape[2]
    anywhere = pl.BlockSpec(memory_space=pl.ANY)
    f32 = jnp.float32
    return pl.pallas_call(
        kernel,
        out_shape=jax.ShapeDtypeStruct(objects.shape, f32),
        in_specs=[pl.BlockSpec(memory_space=pltpu.SMEM)] + [anywhere] * 6,
        out_specs=anywhere,
        scratch_shapes=[
            pltpu.VMEM((2, 3, 384, LANES), f32),
            pltpu.VMEM((2, 3, 384, LANES), f32),
            pltpu.VMEM((2, 2, WIN, WIN), f32),
            pltpu.VMEM((count, 256, 256), f32),
            pltpu.VMEM((WIN, WIN), f32),
            pltpu.VMEM((2, WIN, WIN), f32),
            pltpu.VMEM((4 * count + 1, 640, LANES), f32),
            pltpu.VMEM((2, 2, 3, 384, LANES), f32),
            pltpu.VMEM((2, 2, 3, WIN, LANES), f32),
            pltpu.VMEM((2, 2, 256, LANES), f32),
            pltpu.VMEM((count, WIN, WIN), f32),
            pltpu.VMEM(right.shape, jnp.bfloat16),
            pltpu.VMEM(left.shape, jnp.bfloat16),
            pltpu.SemaphoreType.DMA((16,)),
            pltpu.SemaphoreType.DMA((33,)),
            pltpu.SemaphoreType.DMA((33,)),
        ],
        compiler_params=pltpu.CompilerParams(
            vmem_limit_bytes=60 * 2**20, collective_id=0, has_side_effects=True
        ),
        name="tile_gradient",
    )(offsets, objects, probes, phase, measured, jnp.asarray(right), jnp.asarray(left))


def solution(mesh):
    placed = (
        P(None, None, "row", "col"),
        P("mode", None, None, None),
        P(),
        P("row", "col", None, None),
        P("row", "col", None, None, None),
    )
    return jax.shard_map(
        on_device,
        mesh=mesh,
        in_specs=placed,
        out_specs=P(None, None, "row", "col"),
        check_vma=False,
    )
```

time: 110 us -> 63.3 us (0.58)
  the two profiles are of different devices: /device:TPU:110 before, /device:TPU:140 now
where the time goes in v1:
time: 63.3 us; the launch traced here: 62.2 us
  Pallas kernels  58.6 us (93%)
  local copies, waits for them, and re-layouts  3.63 us (6%)
    pallas_call x1, Pallas kernels, on_device(): pl.pallas_call(kernel, out_shape=jax.ShapeDtypeStruct(objects.shape, f32)...  58.6 us
    unnamed x2, local copies, waits for them, and re-layouts  3.63 us

profile of v1, /device:TPU:140, one launch (start us, length us, event | category | flops | bytes accessed | tf_op | source)
XLA Modules:
  0.0 62.2 jit_solution(6234139601657653153)
XLA Ops:
  0.0 1.3 %copy.8.offsets = s32[1,1,8,2]{3,2,1,0:T(8,128)} copy(s32[1,1,8,2]{2,3,1,0:T(2,128)} %param.10) | data formatting | bytes 128 | tf_op args[3]
  1.3 58.6 %tile_gradient.1 = f32[2,2,256,256]{3,2,1,0:T(8,128)} custom-call(s32[1,1,8,2]{3,2,1,0:T(8,128)} %copy.8.offsets, f32[2,2,256,256]{3,2,1,0:T(8,128)} %objects.1, f32[1,2,128,128]{3,2,1,0:T(8,128)} %probes.1, f32[128,128]{1,0:T(8,128)} %phase.1, f32[1,1,8,128,128]{4,3,2,1,0:T(8,128)} %measured.1, bf16[2,768,256]{2,1,0:T(8,128)(2,1)} %constant.4.clone.right_in, ...), custom_call_target="tpu_custom_call" | custom-call | tf_op jit(solution)/shard_map/tile_gradient/pallas_call | solution.py:448
  59.9 2.3 %copy.10 = f32[2,2,256,256]{3,2,1,0:T(8,128)} copy(f32[2,2,256,256]{3,2,1,0:T(8,128)} %tile_gradient.1) | data formatting | bytes 2097152

commit v2 on v1

--- a/solution.py
+++ b/solution.py
@@ -11,7 +11,6 @@
 
 WIN = 128
 LANES = 128
-STEP = 2
 MESH = pl.DeviceIdType.MESH
 
 
@@ -67,16 +66,6 @@
         (value[:WIN, at : at + WIN], value[WIN:, at : at + WIN])
         for at in range(0, value.shape[1], WIN)
     ]
-
-
-def forward_two(fields, right, left):
-    rows_done = from_beside(along_rows(beside_form(fields), right[0]))
-    return from_stacked(along_columns(stacked_form(rows_done), left[0]))
-
-
-def inverse_two(fields, right, left):
-    columns_done = from_stacked(along_columns(stacked_form(fields), left[1]))
-    return from_beside(along_rows(beside_form(columns_done), right[1]))
 
 
 def times(a, b):
@@ -133,10 +122,10 @@
         copy.start()
 
     barrier = pltpu.get_barrier_semaphore()
-    everyone = (up, down, leftward, rightward, up_left, down_right, partner)
-    for one in everyone:
+    around = (up, down, leftward, rightward, up_left, down_right, partner)
+    for one in around:
         pl.semaphore_signal(barrier, inc=1, device_id=one, device_id_type=MESH)
-    pl.semaphore_wait(barrier, len(everyone))
+    pl.semaphore_wait(barrier, len(around))
 
     def in_low(s, j, which):
         return remote(
@@ -204,6 +193,23 @@
         for s in range(2):
             for c in range(2):
                 ext[s][c, 2, below, :] = jnp.zeros((WIN, LANES), jnp.float32)
+
+    @pl.when(jnp.logical_not(has_left))
+    def _():
+        moved[...] = jnp.zeros_like(moved)
+
+    @pl.when(jnp.logical_not(has_up))
+    def _():
+        for s in range(2):
+            for c in range(2):
+                for j in range(2):
+                    fallen[s, c, j] = jnp.zeros((WIN, LANES), jnp.float32)
+
+    @pl.when(jnp.logical_not(has_up & has_left))
+    def _():
+        for s in range(2):
+            for c in range(2):
+                fallen[s, c, 2] = jnp.zeros((WIN, LANES), jnp.float32)
 
     spread[...] = jnp.zeros_like(spread)
     get_phase.wait()
@@ -267,36 +273,42 @@
                 out_corner(s, mode).wait_recv()
                 out_pass(s, j, mode).start()
 
-    def arrive_out(s):
-        @pl.when(has_left)
-        def _():
-            for c in range(2):
-                out_right(s, c).wait_recv()
-                total[s, c, 0, beside, :] += moved[s, c]
-
-        @pl.when(has_up)
-        def _():
-            for j in range(2):
-                out_pass(s, j, other).wait_recv()
-                for c in range(2):
-                    total[s, c, j, pl.ds(0, WIN), :] += fallen[s, c, j]
-
-        @pl.when(has_up & has_left)
-        def _():
-            out_pass(s, 2, other).wait_recv()
-            for c in range(2):
-                total[s, c, 0, pl.ds(0, WIN), :] += fallen[s, c, 2]
-
     def result(s):
         return [
             fetch(total.at[s, :, j, beside, :], out.at[s, :, :, pl.ds(LANES * j, LANES)], 9 + 2 * s + j)
             for j in range(2)
         ]
 
+    def arrive_out(s):
+        @pl.when(has_left)
+        def _():
+            for c in range(2):
+                out_right(s, c).wait_recv()
+
+        @pl.when(has_up)
+        def _():
+            for j in range(2):
+                out_pass(s, j, other).wait_recv()
+
+        @pl.when(has_up & has_left)
+        def _():
+            out_pass(s, 2, other).wait_recv()
+
+        low = pl.ds(WIN, WIN)
+        for c in range(2):
+            for j in range(2):
+                top = total[s, c, j, pl.ds(0, WIN), :] + fallen[s, c, j]
+                if j == 0:
+                    top = top + moved[s, c, pl.ds(0, WIN), :] + fallen[s, c, 2]
+                    total[s, c, j, low, :] += moved[s, c, low, :]
+                total[s, c, j, pl.ds(0, WIN), :] = top
+        for copy in result(s):
+            copy.start()
+
     lane = lax.broadcasted_iota(jnp.int32, (WIN, LANES), 1)
 
     def window(s, p):
-        r0, c0 = offsets[0, 0, p, 0], offsets[0, 0, p, 1]
+        r0, c0 = offsets[0, 0, 0, p], offsets[0, 0, 1, p]
         tile = c0 // LANES
         shift = c0 % LANES
         back = (LANES - shift) % LANES
@@ -309,7 +321,7 @@
         return part(0), part(1)
 
     def leave(p, patch):
-        shift = offsets[0, 0, p, 1] % LANES
+        shift = offsets[0, 0, 1, p] % LANES
         for c in range(2):
             rolled = pltpu.roll(patch[c], shift, 1)
             spread[4 * p + 2 * c, pl.ds(256, WIN), :] = jnp.where(lane >= shift, rolled, 0.0)
@@ -320,7 +332,7 @@
             for j, at in blocks:
                 value = jnp.zeros((WIN, LANES), jnp.float32)
                 for p in range(count):
-                    r0, tile = offsets[0, 0, p, 0], offsets[0, 0, p, 1] // LANES
+                    r0, tile = offsets[0, 0, 0, p], offsets[0, 0, 1, p] // LANES
                     index = jnp.where(
                         tile == j, 4 * p + 2 * c, jnp.where(tile == j - 1, 4 * p + 2 * c + 1, 4 * count)
                     )
@@ -340,67 +352,71 @@
     modes = [(both[m, 0], both[m, 1]) for m in range(2)]
     passage = (prop[0], prop[1])
 
-    def first_phase(step, _):
-        for j in range(3):
-            @pl.when(step == j + 1)
-            def _(j=j):
-                hand_in(1, j)
-
-        for k in range(STEP):
-            p = step * STEP + k
-            view = window(0, p)
-            spectrum = forward_two([times(mode, view) for mode in modes], right, left)
-            field = inverse_two([times(passage, one) for one in spectrum], right, left)
-            middle[p] = beside_form(field)
-        return 0
-
-    def second_phase(step, _):
-        for k in range(STEP):
-            p = step * STEP + k
-            view = window(1, p)
-            field = from_beside(middle[p])
-            far = forward_two([times(one, view) for one in field], right, left)
-            power = sum(one[0] * one[0] + one[1] * one[1] for one in far)
-            weight = 4.0 * (power - target[p])
-            gexit = inverse_two([(weight * one[0], weight * one[1]) for one in far], right, left)
-            pieces = [times_conj(g, b) for g, b in zip(gexit, field)]
-            leave(p, (pieces[0][0] + pieces[1][0], pieces[0][1] + pieces[1][1]))
-            middle[p] = beside_form([times_conj(g, view) for g in gexit])
-        return 0
-
-    def third_phase(step, _):
-        for j in range(3):
-            @pl.when(step == j + 1)
-            def _(j=j):
-                hand_out(1, j)
-
-        for k in range(STEP):
-            p = step * STEP + k
-            spectrum = forward_two(from_beside(middle[p]), right, left)
-            wave = inverse_two([times_conj(one, passage) for one in spectrum], right, left)
-            pieces = [times_conj(g, mode) for g, mode in zip(wave, modes)]
-            leave(p, (pieces[0][0] + pieces[1][0], pieces[0][1] + pieces[1][1]))
-        return 0
-
-    lax.fori_loop(0, count // STEP, first_phase, 0)
+    everyone = range(count)
+
+    def rows_forward(fields):
+        return from_beside(along_rows(beside_form(fields), right[0]))
+
+    def rows_inverse(fields):
+        return from_beside(along_rows(beside_form(fields), right[1]))
+
+    def columns_forward(fields):
+        return from_stacked(along_columns(stacked_form(fields), left[0]))
+
+    def columns_inverse(fields):
+        return from_stacked(along_columns(stacked_form(fields), left[1]))
+
+    views = [window(0, p) for p in everyone]
+    rows_done = rows_forward([times(one, view) for view in views for one in modes])
+    hand_in(1, 0)
+    spectrum = columns_forward(rows_done)
+    hand_in(1, 1)
+    columns_done = columns_inverse([times(passage, one) for one in spectrum])
+    hand_in(1, 2)
+    field = rows_inverse(columns_done)
+    for p in everyone:
+        middle[p] = beside_form(field[2 * p : 2 * p + 2])
+
     arrive_in(1)
     get_target.wait()
-    lax.fori_loop(0, count // STEP, second_phase, 0)
+
+    views = [window(1, p) for p in everyone for _ in range(2)]
+    field = [one for p in everyone for one in from_beside(middle[p])]
+    far = columns_forward(rows_forward([times(one, view) for one, view in zip(field, views)]))
+    back_far = []
+    for p in everyone:
+        pair = far[2 * p : 2 * p + 2]
+        power = sum(one[0] * one[0] + one[1] * one[1] for one in pair)
+        weight = 4.0 * (power - target[p])
+        back_far += [(weight * one[0], weight * one[1]) for one in pair]
+    back_exit = rows_inverse(columns_inverse(back_far))
+    for p in everyone:
+        pieces = [times_conj(back_exit[q], field[q]) for q in (2 * p, 2 * p + 1)]
+        leave(p, (pieces[0][0] + pieces[1][0], pieces[0][1] + pieces[1][1]))
+        middle[p] = beside_form([times_conj(back_exit[q], views[q]) for q in (2 * p, 2 * p + 1)])
+
     gather(1, rims)
     send_out(1)
     gather(1, inside)
-    lax.fori_loop(0, count // STEP, third_phase, 0)
+
+    rows_done = rows_forward([one for p in everyone for one in from_beside(middle[p])])
+    spectrum = columns_forward(rows_done)
+    hand_out(1, 0)
+    columns_done = columns_inverse([times_conj(one, passage) for one in spectrum])
+    hand_out(1, 1)
+    wave = rows_inverse(columns_done)
+    hand_out(1, 2)
+    for p in everyone:
+        pieces = [times_conj(wave[2 * p + m], modes[m]) for m in range(2)]
+        leave(p, (pieces[0][0] + pieces[1][0], pieces[0][1] + pieces[1][1]))
+
     gather(0, rims)
     send_out(0)
     gather(0, inside)
     arrive_out(1)
-    for copy in result(1):
-        copy.start()
     for j in range(3):
         hand_out(0, j)
     arrive_out(0)
-    for copy in result(0):
-        copy.start()
 
     share.wait_send()
     for s in range(2):
@@ -464,7 +480,7 @@
             pltpu.VMEM((count, WIN, WIN), f32),
             pltpu.VMEM(right.shape, jnp.bfloat16),
             pltpu.VMEM(left.shape, jnp.bfloat16),
-            pltpu.SemaphoreType.DMA((16,)),
+            pltpu.SemaphoreType.DMA((13,)),
             pltpu.SemaphoreType.DMA((33,)),
             pltpu.SemaphoreType.DMA((33,)),
         ],
@@ -472,7 +488,7 @@
             vmem_limit_bytes=60 * 2**20, collective_id=0, has_side_effects=True
         ),
         name="tile_gradient",
-    )(offsets, objects, probes, phase, measured, jnp.asarray(right), jnp.asarray(left))
+    )(jnp.swapaxes(offsets, 2, 3), objects, probes, phase, measured, jnp.asarray(right), jnp.asarray(left))
 
 
 def solution(mesh):

time: 63.3 us -> 51.4 us (0.81)
  the two profiles are of different devices: /device:TPU:140 before, /device:TPU:42 now
where the time goes in v2:
time: 51.4 us; the launch traced here: 51.3 us
  Pallas kernels  49 us (95%)
  local copies, waits for them, and re-layouts  2.29 us (4%)
    pallas_call x1, Pallas kernels, on_device(): pl.pallas_call(kernel, out_shape=jax.ShapeDtypeStruct(objects.shape, f32)...  49 us
    unnamed x1, local copies, waits for them, and re-layouts  2.29 us

profile of v2, /device:TPU:42, one launch (start us, length us, event | category | flops | bytes accessed | tf_op | source)
XLA Modules:
  0.0 51.3 jit_solution(10542583871101363352)
XLA Ops:
  0.0 49.0 %tile_gradient.1 = f32[2,2,256,256]{3,2,1,0:T(8,128)} custom-call(s32[1,1,2,8]{3,2,1,0:T(2,128)} %bitcast.1, f32[2,2,256,256]{3,2,1,0:T(8,128)} %objects.1, f32[1,2,128,128]{3,2,1,0:T(8,128)} %probes.1, f32[128,128]{1,0:T(8,128)} %phase.1, f32[1,1,8,128,128]{4,3,2,1,0:T(8,128)} %measured.1, bf16[2,768,256]{2,1,0:T(8,128)(2,1)} %constant.4.clone.right_in, ...), custom_call_target="tpu_custom_call" | custom-call | tf_op jit(solution)/shard_map/tile_gradient/pallas_call | solution.py:464
  49.0 2.3 %copy.9 = f32[2,2,256,256]{3,2,1,0:T(8,128)} copy(f32[2,2,256,256]{3,2,1,0:T(8,128)} %tile_gradient.1) | data formatting | bytes 2097152

commit v3 on v2

--- a/solution.py
+++ b/solution.py
@@ -13,6 +13,9 @@
 LANES = 128
 MESH = pl.DeviceIdType.MESH
 
+CHUNKS_FIRST = ((0, 0, 128), (1, 0, 64), (1, 64, 64))
+CHUNKS_SECOND = ((0, 0, 128), (1, 0, 64), (1, 64, 64))
+
 
 def fourier_tables():
     counter = np.arange(WIN)
@@ -79,7 +82,7 @@
 def kernel(
     offsets, objects, probes, phase, measured, right_in, left_in,
     out,
-    ext_first, ext_second, both, middle, angle, prop, spread, total, fallen, moved, target, right, left,
+    ext_first, ext_second, both, middle, angle, prop, spread_first, spread_second, total, fallen, moved, target, right, left,
     sems, send, recv,
 ):
     rows, cols = lax.axis_size("row"), lax.axis_size("col")
@@ -106,6 +109,9 @@
 
     below, beside = pl.ds(256, WIN), pl.ds(0, 256)
     ext = (ext_first, ext_second)
+    spread = (spread_first, spread_second)
+    chunks = (CHUNKS_FIRST, CHUNKS_SECOND)
+    direct = tuple([j for j in range(3) if all(chunk[0] != j for chunk in part)] for part in chunks)
 
     own = [
         [fetch(objects.at[s, :, :, pl.ds(LANES * j, LANES)], ext[s].at[:, j, beside, :], 2 * s + j) for j in range(2)]
@@ -122,55 +128,81 @@
         copy.start()
 
     barrier = pltpu.get_barrier_semaphore()
-    around = (up, down, leftward, rightward, up_left, down_right, partner)
-    for one in around:
-        pl.semaphore_signal(barrier, inc=1, device_id=one, device_id_type=MESH)
-    pl.semaphore_wait(barrier, len(around))
-
-    def in_low(s, j, which):
-        return remote(
-            objects.at[s, which, pl.ds(0, WIN), pl.ds(LANES * j, LANES)], ext[s].at[which, j, below, :], 8 * s + j, up
+    number = jnp.int32(1)
+    pl.semaphore_signal(barrier, inc=1, device_id=partner, device_id_type=MESH)
+    for one, there in ((down, has_down), (rightward, has_right), (down_right, has_down & has_right)):
+        @pl.when(there)
+        def _(one=one):
+            pl.semaphore_signal(barrier, inc=1, device_id=one, device_id_type=MESH)
+    for there in (has_up, has_left, has_up & has_left):
+        number += there.astype(jnp.int32)
+    pl.semaphore_wait(barrier, number)
+
+    known = {}
+
+    def linked(name, src, dst, to):
+        return remote(src, dst, known.setdefault(name, len(known)), to)
+
+    def in_low(s, chunk, which):
+        j, at, size = chunk
+        src = objects.at[s, which, pl.ds(at, size), pl.ds(LANES * (j % 2), LANES)]
+        return linked(("in", s, chunk), src, ext[s].at[which, j, pl.ds(256 + at, size), :], up_left if j == 2 else up)
+
+    def in_direct(s, j, c):
+        src = objects.at[s, c, pl.ds(0, WIN), pl.ds(LANES * (j % 2), LANES)]
+        return linked(("in direct", s, j, c), src, ext[s].at[c, j, below, :], up_left if j == 2 else up)
+
+    def in_right(s, c):
+        return linked(
+            ("in right", s, c), objects.at[s, c, :, pl.ds(0, LANES)], ext[s].at[c, 2, beside, :], leftward
         )
 
-    def in_corner(s, which):
-        return remote(
-            objects.at[s, which, pl.ds(0, WIN), pl.ds(0, LANES)], ext[s].at[which, 2, below, :], 8 * s + 2, up_left
+    def in_pass(s, chunk, which):
+        j, at, size = chunk
+        part = ext[s].at[which, j, pl.ds(256 + at, size), :]
+        return linked(("in pass", s, chunk), part, part, partner)
+
+    share = linked("share", probes.at[0], both.at[mode], partner)
+
+    def out_low(s, chunk, which):
+        j, at, size = chunk
+        src = total.at[s, which, j, pl.ds(256 + at, size), :]
+        return linked(
+            ("out", s, chunk), src, fallen.at[s, which, j, pl.ds(at, size), :], down_right if j == 2 else down
         )
 
-    def in_right(s, c):
-        return remote(objects.at[s, c, :, pl.ds(0, LANES)], ext[s].at[c, 2, beside, :], 8 * s + 3 + c, leftward)
-
-    def in_pass(s, j, which):
-        return remote(ext[s].at[which, j, below, :], ext[s].at[which, j, below, :], 8 * s + 5 + j, partner)
-
-    share = remote(probes.at[0], both.at[mode], 32, partner)
-
-    def out_low(s, j, which):
-        return remote(total.at[s, which, j, below, :], fallen.at[s, which, j], 16 + 8 * s + j, down)
-
-    def out_corner(s, which):
-        return remote(total.at[s, which, 2, below, :], fallen.at[s, which, 2], 16 + 8 * s + 2, down_right)
+    def out_direct(s, j, c):
+        return linked(
+            ("out direct", s, j, c), total.at[s, c, j, below, :], fallen.at[s, c, j], down_right if j == 2 else down
+        )
 
     def out_right(s, c):
-        return remote(total.at[s, c, 2, beside, :], moved.at[s, c], 16 + 8 * s + 3 + c, rightward)
-
-    def out_pass(s, j, which):
-        return remote(fallen.at[s, which, j], fallen.at[s, which, j], 16 + 8 * s + 5 + j, partner)
+        return linked(("out right", s, c), total.at[s, c, 2, beside, :], moved.at[s, c], rightward)
+
+    def out_pass(s, chunk, which):
+        j, at, size = chunk
+        part = fallen.at[s, which, j, pl.ds(at, size), :]
+        return linked(("out pass", s, chunk), part, part, partner)
+
+    def crossing(j, vertical, sideways):
+        return vertical & sideways if j == 2 else vertical
 
     for s in range(2):
-        @pl.when(has_up)
-        def _(s=s):
-            for j in range(2):
-                in_low(s, j, other).start()
+        for chunk in chunks[s]:
+            @pl.when(crossing(chunk[0], has_up, has_left))
+            def _(s=s, chunk=chunk):
+                in_low(s, chunk, other).start()
 
         @pl.when(has_left)
         def _(s=s):
             for c in range(2):
                 in_right(s, c).start()
 
-        @pl.when(has_up & has_left)
-        def _(s=s):
-            in_corner(s, other).start()
+        for j in direct[s]:
+            @pl.when(crossing(j, has_up, has_left))
+            def _(s=s, j=j):
+                for c in range(2):
+                    in_direct(s, j, c).start()
 
         if s == 0:
             share.start()
@@ -211,22 +243,21 @@
             for c in range(2):
                 fallen[s, c, 2] = jnp.zeros((WIN, LANES), jnp.float32)
 
-    spread[...] = jnp.zeros_like(spread)
+    for one in spread:
+        one[...] = jnp.zeros_like(one)
     get_phase.wait()
     prop[0] = jnp.cos(angle[...])
     prop[1] = jnp.sin(angle[...])
 
-    def hand_in(s, j):
-        if j < 2:
-            @pl.when(has_down)
-            def _():
-                in_low(s, j, mode).wait_recv()
-                in_pass(s, j, mode).start()
-        else:
-            @pl.when(has_down & has_right)
-            def _():
-                in_corner(s, mode).wait_recv()
-                in_pass(s, j, mode).start()
+    def hand_in(s, at):
+        if at >= len(chunks[s]):
+            return
+        chunk = chunks[s][at]
+
+        @pl.when(crossing(chunk[0], has_down, has_right))
+        def _():
+            in_low(s, chunk, mode).wait_recv()
+            in_pass(s, chunk, mode).start()
 
     def arrive_in(s):
         for copy in own[s]:
@@ -237,41 +268,43 @@
             for c in range(2):
                 in_right(s, c).wait_recv()
 
-        @pl.when(has_down)
-        def _():
-            for j in range(2):
-                in_pass(s, j, other).wait_recv()
-
-        @pl.when(has_down & has_right)
-        def _():
-            in_pass(s, 2, other).wait_recv()
+        for chunk in chunks[s]:
+            @pl.when(crossing(chunk[0], has_down, has_right))
+            def _(chunk=chunk):
+                in_pass(s, chunk, other).wait_recv()
+
+        for j in direct[s]:
+            @pl.when(crossing(j, has_down, has_right))
+            def _(j=j):
+                for c in range(2):
+                    in_direct(s, j, c).wait_recv()
 
     def send_out(s):
-        @pl.when(has_down)
-        def _():
-            for j in range(2):
-                out_low(s, j, other).start()
+        for chunk in chunks[s]:
+            @pl.when(crossing(chunk[0], has_down, has_right))
+            def _(chunk=chunk):
+                out_low(s, chunk, other).start()
 
         @pl.when(has_right)
         def _():
             for c in range(2):
                 out_right(s, c).start()
 
-        @pl.when(has_down & has_right)
+        for j in direct[s]:
+            @pl.when(crossing(j, has_down, has_right))
+            def _(j=j):
+                for c in range(2):
+                    out_direct(s, j, c).start()
+
+    def hand_out(s, at):
+        if at >= len(chunks[s]):
+            return
+        chunk = chunks[s][at]
+
+        @pl.when(crossing(chunk[0], has_up, has_left))
         def _():
-            out_corner(s, other).start()
-
-    def hand_out(s, j):
-        if j < 2:
-            @pl.when(has_up)
-            def _():
-                out_low(s, j, mode).wait_recv()
-                out_pass(s, j, mode).start()
-        else:
-            @pl.when(has_up & has_left)
-            def _():
-                out_corner(s, mode).wait_recv()
-                out_pass(s, j, mode).start()
+            out_low(s, chunk, mode).wait_recv()
+            out_pass(s, chunk, mode).start()
 
     def result(s):
         return [
@@ -285,14 +318,16 @@
             for c in range(2):
                 out_right(s, c).wait_recv()
 
-        @pl.when(has_up)
-        def _():
-            for j in range(2):
-                out_pass(s, j, other).wait_recv()
-
-        @pl.when(has_up & has_left)
-        def _():
-            out_pass(s, 2, other).wait_recv()
+        for chunk in chunks[s]:
+            @pl.when(crossing(chunk[0], has_up, has_left))
+            def _(chunk=chunk):
+                out_pass(s, chunk, other).wait_recv()
+
+        for j in direct[s]:
+            @pl.when(crossing(j, has_up, has_left))
+            def _(j=j):
+                for c in range(2):
+                    out_direct(s, j, c).wait_recv()
 
         low = pl.ds(WIN, WIN)
         for c in range(2):
@@ -320,12 +355,12 @@
 
         return part(0), part(1)
 
-    def leave(p, patch):
+    def leave(s, p, patch):
         shift = offsets[0, 0, 1, p] % LANES
         for c in range(2):
             rolled = pltpu.roll(patch[c], shift, 1)
-            spread[4 * p + 2 * c, pl.ds(256, WIN), :] = jnp.where(lane >= shift, rolled, 0.0)
-            spread[4 * p + 2 * c + 1, pl.ds(256, WIN), :] = jnp.where(lane < shift, rolled, 0.0)
+            spread[s][4 * p + 2 * c, pl.ds(256, WIN), :] = jnp.where(lane >= shift, rolled, 0.0)
+            spread[s][4 * p + 2 * c + 1, pl.ds(256, WIN), :] = jnp.where(lane < shift, rolled, 0.0)
 
     def gather(s, blocks):
         for c in range(2):
@@ -336,14 +371,14 @@
                     index = jnp.where(
                         tile == j, 4 * p + 2 * c, jnp.where(tile == j - 1, 4 * p + 2 * c + 1, 4 * count)
                     )
-                    value += spread[index, pl.ds(256 - r0 + WIN * at, WIN), :]
+                    value += spread[s][index, pl.ds(256 - r0 + WIN * at, WIN), :]
                 total[s, c, j, pl.ds(WIN * at, WIN), :] = value
 
     rims = [(0, 2), (1, 2), (2, 2), (2, 0), (2, 1)]
     inside = [(0, 0), (0, 1), (1, 0), (1, 1)]
 
-    for j in range(3):
-        hand_in(0, j)
+    for at in range(len(chunks[0])):
+        hand_in(0, at)
     for copy in needed:
         copy.wait()
     share.wait_recv()
@@ -392,12 +427,11 @@
     back_exit = rows_inverse(columns_inverse(back_far))
     for p in everyone:
         pieces = [times_conj(back_exit[q], field[q]) for q in (2 * p, 2 * p + 1)]
-        leave(p, (pieces[0][0] + pieces[1][0], pieces[0][1] + pieces[1][1]))
+        leave(1, p, (pieces[0][0] + pieces[1][0], pieces[0][1] + pieces[1][1]))
         middle[p] = beside_form([times_conj(back_exit[q], views[q]) for q in (2 * p, 2 * p + 1)])
 
     gather(1, rims)
     send_out(1)
-    gather(1, inside)
 
     rows_done = rows_forward([one for p in everyone for one in from_beside(middle[p])])
     spectrum = columns_forward(rows_done)
@@ -408,49 +442,50 @@
     hand_out(1, 2)
     for p in everyone:
         pieces = [times_conj(wave[2 * p + m], modes[m]) for m in range(2)]
-        leave(p, (pieces[0][0] + pieces[1][0], pieces[0][1] + pieces[1][1]))
+        leave(0, p, (pieces[0][0] + pieces[1][0], pieces[0][1] + pieces[1][1]))
 
     gather(0, rims)
     send_out(0)
+    gather(1, inside)
     gather(0, inside)
     arrive_out(1)
-    for j in range(3):
-        hand_out(0, j)
+    for at in range(len(chunks[0])):
+        hand_out(0, at)
     arrive_out(0)
 
     share.wait_send()
     for s in range(2):
-        @pl.when(has_up)
-        def _(s=s):
-            for j in range(2):
-                in_low(s, j, other).wait_send()
-                out_pass(s, j, mode).wait_send()
+        for chunk in chunks[s]:
+            @pl.when(crossing(chunk[0], has_up, has_left))
+            def _(s=s, chunk=chunk):
+                in_low(s, chunk, other).wait_send()
+                out_pass(s, chunk, mode).wait_send()
+
+            @pl.when(crossing(chunk[0], has_down, has_right))
+            def _(s=s, chunk=chunk):
+                in_pass(s, chunk, mode).wait_send()
+                out_low(s, chunk, other).wait_send()
 
         @pl.when(has_left)
         def _(s=s):
             for c in range(2):
                 in_right(s, c).wait_send()
 
-        @pl.when(has_up & has_left)
-        def _(s=s):
-            in_corner(s, other).wait_send()
-            out_pass(s, 2, mode).wait_send()
-
-        @pl.when(has_down)
-        def _(s=s):
-            for j in range(2):
-                in_pass(s, j, mode).wait_send()
-                out_low(s, j, other).wait_send()
-
         @pl.when(has_right)
         def _(s=s):
             for c in range(2):
                 out_right(s, c).wait_send()
 
-        @pl.when(has_down & has_right)
-        def _(s=s):
-            in_pass(s, 2, mode).wait_send()
-            out_corner(s, other).wait_send()
+        for j in direct[s]:
+            @pl.when(crossing(j, has_up, has_left))
+            def _(s=s, j=j):
+                for c in range(2):
+                    in_direct(s, j, c).wait_send()
+
+            @pl.when(crossing(j, has_down, has_right))
+            def _(s=s, j=j):
+                for c in range(2):
+                    out_direct(s, j, c).wait_send()
 
         for copy in result(s):
             copy.wait()
@@ -474,6 +509,7 @@
             pltpu.VMEM((WIN, WIN), f32),
             pltpu.VMEM((2, WIN, WIN), f32),
             pltpu.VMEM((4 * count + 1, 640, LANES), f32),
+            pltpu.VMEM((4 * count + 1, 640, LANES), f32),
             pltpu.VMEM((2, 2, 3, 384, LANES), f32),
             pltpu.VMEM((2, 2, 3, WIN, LANES), f32),
             pltpu.VMEM((2, 2, 256, LANES), f32),
@@ -481,8 +517,8 @@
             pltpu.VMEM(right.shape, jnp.bfloat16),
             pltpu.VMEM(left.shape, jnp.bfloat16),
             pltpu.SemaphoreType.DMA((13,)),
-            pltpu.SemaphoreType.DMA((33,)),
-            pltpu.SemaphoreType.DMA((33,)),
+            pltpu.SemaphoreType.DMA((64,)),
+            pltpu.SemaphoreType.DMA((64,)),
         ],
         compiler_params=pltpu.CompilerParams(
             vmem_limit_bytes=60 * 2**20, collective_id=0, has_side_effects=True

time: 51.4 us -> 46.3 us (0.901)
  the two profiles are of different devices: /device:TPU:42 before, /device:TPU:140 now
where the time goes in v3:
time: 46.3 us; the launch traced here: 46.2 us
  Pallas kernels  43.9 us (95%)
  local copies, waits for them, and re-layouts  2.29 us (5%)
    pallas_call x1, Pallas kernels, on_device(): pl.pallas_call(kernel, out_shape=jax.ShapeDtypeStruct(objects.shape, f32)...  43.9 us
    unnamed x1, local copies, waits for them, and re-layouts  2.29 us

profile of v3, /device:TPU:140, one launch (start us, length us, event | category | flops | bytes accessed | tf_op | source)
XLA Modules:
  0.0 46.2 jit_solution(6085077392562428498)
XLA Ops:
  0.0 43.9 %tile_gradient.1 = f32[2,2,256,256]{3,2,1,0:T(8,128)} custom-call(s32[1,1,2,8]{3,2,1,0:T(2,128)} %bitcast.1, f32[2,2,256,256]{3,2,1,0:T(8,128)} %objects.1, f32[1,2,128,128]{3,2,1,0:T(8,128)} %probes.1, f32[128,128]{1,0:T(8,128)} %phase.1, f32[1,1,8,128,128]{4,3,2,1,0:T(8,128)} %measured.1, bf16[2,768,256]{2,1,0:T(8,128)(2,1)} %constant.4.clone.right_in, ...), custom_call_target="tpu_custom_call" | custom-call | tf_op jit(solution)/shard_map/tile_gradient/pallas_call | solution.py:499
  43.9 2.3 %copy.9 = f32[2,2,256,256]{3,2,1,0:T(8,128)} copy(f32[2,2,256,256]{3,2,1,0:T(8,128)} %tile_gradient.1) | data formatting | bytes 2097152

commit v4 on v3

--- a/solution.py
+++ b/solution.py
@@ -11,6 +11,7 @@
 
 WIN = 128
 LANES = 128
+HALF = WIN // 2
 MESH = pl.DeviceIdType.MESH
 
 CHUNKS_FIRST = ((0, 0, 128), (1, 0, 64), (1, 64, 64))
@@ -27,10 +28,18 @@
         high = matrix.astype(jnp.bfloat16)
         return high, (matrix - high.astype(np.float64)).astype(jnp.bfloat16)
 
-    f_high, f_low = parts(forward)
-    i_high, i_low = parts(forward.T)
-    right = np.stack([np.concatenate([f_high, f_high, f_low], 0), np.concatenate([i_high, i_high, i_low], 0)])
-    left = np.stack([np.concatenate([i_high, i_high, i_low], 1), np.concatenate([f_high, f_high, f_low], 1)])
+    def for_rows(matrix):
+        high, low = parts(matrix)
+        return np.concatenate([high, high, low], 0)
+
+    def for_columns(sign):
+        angle = 2.0 * math.pi * (np.outer(np.arange(HALF), np.arange(HALF)) % HALF) / HALF
+        table_re, table_im = np.cos(angle) / math.sqrt(WIN), -sign * np.sin(angle) / math.sqrt(WIN)
+        high, low = parts(np.block([[table_re, -table_im], [table_im, table_re]]))
+        return np.block([[high, high], [low, low]])
+
+    right = np.stack([for_rows(forward), for_rows(forward.T)])
+    left = np.stack([for_columns(1.0), for_columns(-1.0)])
     return right, left
 
 
@@ -44,17 +53,17 @@
     return jnp.dot(jnp.concatenate([high, low, high], 1), table, preferred_element_type=jnp.float32)
 
 
-def along_columns(value, table):
-    high, low = halves(value)
-    return jnp.dot(table, jnp.concatenate([high, low, high], 0), preferred_element_type=jnp.float32)
+def along_columns(pieces, table):
+    value = jnp.concatenate([jnp.concatenate(piece, 0) for piece in pieces], 1)
+    both = jnp.dot(table, jnp.concatenate(halves(value), 0), preferred_element_type=jnp.float32)
+    both = both[:WIN] + both[WIN:]
+    return [
+        (both[:HALF, at : at + WIN], both[HALF:, at : at + WIN]) for at in range(0, value.shape[1], WIN)
+    ]
 
 
 def beside_form(fields):
     return jnp.concatenate([jnp.concatenate(pair, 1) for pair in fields], 0)
-
-
-def stacked_form(fields):
-    return jnp.concatenate([jnp.concatenate(pair, 0) for pair in fields], 1)
 
 
 def from_beside(value):
@@ -64,13 +73,6 @@
     ]
 
 
-def from_stacked(value):
-    return [
-        (value[:WIN, at : at + WIN], value[WIN:, at : at + WIN])
-        for at in range(0, value.shape[1], WIN)
-    ]
-
-
 def times(a, b):
     return a[0] * b[0] - a[1] * b[1], a[0] * b[1] + a[1] * b[0]
 
@@ -82,7 +84,7 @@
 def kernel(
     offsets, objects, probes, phase, measured, right_in, left_in,
     out,
-    ext_first, ext_second, both, middle, angle, prop, spread_first, spread_second, total, fallen, moved, target, right, left,
+    ext_first, ext_second, both, middle, angle, prop, twist, spread_first, spread_second, total, fallen, moved, target, right, left,
     sems, send, recv,
 ):
     rows, cols = lax.axis_size("row"), lax.axis_size("col")
@@ -246,8 +248,13 @@
     for one in spread:
         one[...] = jnp.zeros_like(one)
     get_phase.wait()
-    prop[0] = jnp.cos(angle[...])
-    prop[1] = jnp.sin(angle[...])
+    for at in range(2):
+        view = angle[pl.ds(at, HALF, stride=2), :]
+        prop[0, pl.ds(HALF * at, HALF), :] = jnp.cos(view)
+        prop[1, pl.ds(HALF * at, HALF), :] = jnp.sin(view)
+    turned = lax.broadcasted_iota(jnp.int32, (HALF, WIN), 0).astype(jnp.float32) * (2.0 * math.pi / WIN)
+    twist[0] = jnp.cos(turned)
+    twist[1] = -jnp.sin(turned)
 
     def hand_in(s, at):
         if at >= len(chunks[s]):
@@ -280,21 +287,26 @@
                     in_direct(s, j, c).wait_recv()
 
     def send_out(s):
-        for chunk in chunks[s]:
-            @pl.when(crossing(chunk[0], has_down, has_right))
-            def _(chunk=chunk):
-                out_low(s, chunk, other).start()
+        for j in range(3):
+            gather(s, [(j, 2)])
+            for chunk in chunks[s]:
+                if chunk[0] == j:
+                    @pl.when(crossing(j, has_down, has_right))
+                    def _(chunk=chunk):
+                        out_low(s, chunk, other).start()
+
+            if j in direct[s]:
+                @pl.when(crossing(j, has_down, has_right))
+                def _(j=j):
+                    for c in range(2):
+                        out_direct(s, j, c).start()
+
+        gather(s, [(2, 0), (2, 1)])
 
         @pl.when(has_right)
         def _():
             for c in range(2):
                 out_right(s, c).start()
-
-        for j in direct[s]:
-            @pl.when(crossing(j, has_down, has_right))
-            def _(j=j):
-                for c in range(2):
-                    out_direct(s, j, c).start()
 
     def hand_out(s, at):
         if at >= len(chunks[s]):
@@ -374,7 +386,6 @@
                     value += spread[s][index, pl.ds(256 - r0 + WIN * at, WIN), :]
                 total[s, c, j, pl.ds(WIN * at, WIN), :] = value
 
-    rims = [(0, 2), (1, 2), (2, 2), (2, 0), (2, 1)]
     inside = [(0, 0), (0, 1), (1, 0), (1, 1)]
 
     for at in range(len(chunks[0])):
@@ -396,10 +407,25 @@
         return from_beside(along_rows(beside_form(fields), right[1]))
 
     def columns_forward(fields):
-        return from_stacked(along_columns(stacked_form(fields), left[0]))
+        turn = (twist[0], twist[1])
+        pieces = []
+        for re, im in fields:
+            pieces.append((re[:HALF] + re[HALF:], im[:HALF] + im[HALF:]))
+            pieces.append(times((re[:HALF] - re[HALF:], im[:HALF] - im[HALF:]), turn))
+        done = along_columns(pieces, left[0])
+        return [
+            tuple(jnp.concatenate([even, odd], 0) for even, odd in zip(*done[at : at + 2]))
+            for at in range(0, len(done), 2)
+        ]
 
     def columns_inverse(fields):
-        return from_stacked(along_columns(stacked_form(fields), left[1]))
+        turn = (twist[0], twist[1])
+        done = along_columns([(re[at : at + HALF], im[at : at + HALF]) for re, im in fields for at in (0, HALF)], left[1])
+        out = []
+        for at in range(0, len(done), 2):
+            turned = times_conj(done[at + 1], turn)
+            out.append(tuple(jnp.concatenate([e + o, e - o], 0) for e, o in zip(done[at], turned)))
+        return out
 
     views = [window(0, p) for p in everyone]
     rows_done = rows_forward([times(one, view) for view in views for one in modes])
@@ -422,7 +448,8 @@
     for p in everyone:
         pair = far[2 * p : 2 * p + 2]
         power = sum(one[0] * one[0] + one[1] * one[1] for one in pair)
-        weight = 4.0 * (power - target[p])
+        wanted = jnp.concatenate([target[p, pl.ds(at, HALF, stride=2), :] for at in range(2)], 0)
+        weight = 4.0 * (power - wanted)
         back_far += [(weight * one[0], weight * one[1]) for one in pair]
     back_exit = rows_inverse(columns_inverse(back_far))
     for p in everyone:
@@ -430,7 +457,6 @@
         leave(1, p, (pieces[0][0] + pieces[1][0], pieces[0][1] + pieces[1][1]))
         middle[p] = beside_form([times_conj(back_exit[q], views[q]) for q in (2 * p, 2 * p + 1)])
 
-    gather(1, rims)
     send_out(1)
 
     rows_done = rows_forward([one for p in everyone for one in from_beside(middle[p])])
@@ -444,7 +470,6 @@
         pieces = [times_conj(wave[2 * p + m], modes[m]) for m in range(2)]
         leave(0, p, (pieces[0][0] + pieces[1][0], pieces[0][1] + pieces[1][1]))
 
-    gather(0, rims)
     send_out(0)
     gather(1, inside)
     gather(0, inside)
@@ -508,6 +533,7 @@
             pltpu.VMEM((count, 256, 256), f32),
             pltpu.VMEM((WIN, WIN), f32),
             pltpu.VMEM((2, WIN, WIN), f32),
+            pltpu.VMEM((2, HALF, WIN), f32),
             pltpu.VMEM((4 * count + 1, 640, LANES), f32),
             pltpu.VMEM((4 * count + 1, 640, LANES), f32),
             pltpu.VMEM((2, 2, 3, 384, LANES), f32),

time: 46.3 us -> 44.5 us (0.961)
  Pallas kernels: 43.9 us -> 42.1 us
    pallas_call x1, Pallas kernels: 43.9 us -> 42.1 us  [on_device(): pl.pallas_call(kernel, out_shape=jax.ShapeDtypeStruct(objects.shape, f32)...]
where the time goes in v4:
time: 44.5 us; the launch traced here: 44.4 us
  Pallas kernels  42.1 us (95%)
  local copies, waits for them, and re-layouts  2.29 us (5%)
    pallas_call x1, Pallas kernels, on_device(): pl.pallas_call(kernel, out_shape=jax.ShapeDtypeStruct(objects.shape, f32)...  42.1 us
    unnamed x1, local copies, waits for them, and re-layouts  2.29 us

profile of v4, /device:TPU:140, one launch (start us, length us, event | category | flops | bytes accessed | tf_op | source)
XLA Modules:
  0.0 44.4 jit_solution(16911230421149148782)
XLA Ops:
  0.0 42.1 %tile_gradient.1 = f32[2,2,256,256]{3,2,1,0:T(8,128)} custom-call(s32[1,1,2,8]{3,2,1,0:T(2,128)} %bitcast.1, f32[2,2,256,256]{3,2,1,0:T(8,128)} %objects.1, f32[1,2,128,128]{3,2,1,0:T(8,128)} %probes.1, f32[128,128]{1,0:T(8,128)} %phase.1, f32[1,1,8,128,128]{4,3,2,1,0:T(8,128)} %measured.1, bf16[2,768,256]{2,1,0:T(8,128)(2,1)} %constant.4.clone.right_in, ...), custom_call_target="tpu_custom_call" | custom-call | tf_op jit(solution)/shard_map/tile_gradient/pallas_call | solution.py:524
  42.1 2.3 %copy.9 = f32[2,2,256,256]{3,2,1,0:T(8,128)} copy(f32[2,2,256,256]{3,2,1,0:T(8,128)} %tile_gradient.1) | data formatting | bytes 2097152

commit v5 on v4

--- a/solution.py
+++ b/solution.py
@@ -428,12 +428,13 @@
         return out
 
     views = [window(0, p) for p in everyone]
-    rows_done = rows_forward([times(one, view) for view in views for one in modes])
+    waves = [times(one, view) for view in views for one in modes]
     hand_in(1, 0)
+    rows_done = rows_forward(waves)
+    hand_in(1, 1)
     spectrum = columns_forward(rows_done)
-    hand_in(1, 1)
+    hand_in(1, 2)
     columns_done = columns_inverse([times(passage, one) for one in spectrum])
-    hand_in(1, 2)
     field = rows_inverse(columns_done)
     for p in everyone:
         middle[p] = beside_form(field[2 * p : 2 * p + 2])
@@ -461,16 +462,15 @@
 
     rows_done = rows_forward([one for p in everyone for one in from_beside(middle[p])])
     spectrum = columns_forward(rows_done)
-    hand_out(1, 0)
     columns_done = columns_inverse([times_conj(one, passage) for one in spectrum])
-    hand_out(1, 1)
     wave = rows_inverse(columns_done)
-    hand_out(1, 2)
     for p in everyone:
         pieces = [times_conj(wave[2 * p + m], modes[m]) for m in range(2)]
         leave(0, p, (pieces[0][0] + pieces[1][0], pieces[0][1] + pieces[1][1]))
 
     send_out(0)
+    for at in range(len(chunks[1])):
+        hand_out(1, at)
     gather(1, inside)
     gather(0, inside)
     arrive_out(1)
@@ -516,12 +516,25 @@
             copy.wait()
 
 
+def settle(src, out, held, sems):
+    parts = [(s, c) for s in range(2) for c in range(2)]
+    into = [pltpu.make_async_copy(src.at[part], held.at[part], sems.at[k]) for k, part in enumerate(parts)]
+    away = [pltpu.make_async_copy(held.at[part], out.at[part], sems.at[4 + k]) for k, part in enumerate(parts)]
+    for copy in into:
+        copy.start()
+    for one, copy in zip(into, away):
+        one.wait()
+        copy.start()
+    for copy in away:
+        copy.wait()
+
+
 def on_device(objects, probes, phase, offsets, measured):
     right, left = fourier_tables()
     count = measured.shape[2]
     anywhere = pl.BlockSpec(memory_space=pl.ANY)
     f32 = jnp.float32
-    return pl.pallas_call(
+    gradient = pl.pallas_call(
         kernel,
         out_shape=jax.ShapeDtypeStruct(objects.shape, f32),
         in_specs=[pl.BlockSpec(memory_space=pltpu.SMEM)] + [anywhere] * 6,
@@ -551,6 +564,15 @@
         ),
         name="tile_gradient",
     )(jnp.swapaxes(offsets, 2, 3), objects, probes, phase, measured, jnp.asarray(right), jnp.asarray(left))
+    return pl.pallas_call(
+        settle,
+        out_shape=jax.ShapeDtypeStruct(objects.shape, f32),
+        in_specs=[anywhere],
+        out_specs=anywhere,
+        scratch_shapes=[pltpu.VMEM(objects.shape, f32), pltpu.SemaphoreType.DMA((8,))],
+        compiler_params=pltpu.CompilerParams(vmem_limit_bytes=60 * 2**20),
+        name="settle",
+    )(gradient)
 
 
 def solution(mesh):

time: 44.5 us -> 43.3 us (0.973)
  the two profiles are of different devices: /device:TPU:140 before, /device:TPU:100 now
where the time goes in v5:
time: 43.3 us; the launch traced here: 43.1 us
  Pallas kernels  43 us (99%)
    pallas_call x1, Pallas kernels, on_device(): pl.pallas_call(kernel, out_shape=jax.ShapeDtypeStruct(objects.shape, f32)...  41 us
    pallas_call x1, Pallas kernels, on_device(): pl.pallas_call(settle, out_shape=jax.ShapeDtypeStruct(objects.shape, f32)...  1.98 us

profile of v5, /device:TPU:100, one launch (start us, length us, event | category | flops | bytes accessed | tf_op | source)
XLA Modules:
  0.0 43.1 jit_solution(6330206949362618243)
XLA Ops:
  0.0 41.0 %tile_gradient.1.src = f32[2,2,256,256]{3,2,1,0:T(8,128)} custom-call(s32[1,1,2,8]{3,2,1,0:T(2,128)} %bitcast.1, f32[2,2,256,256]{3,2,1,0:T(8,128)} %objects.1, f32[1,2,128,128]{3,2,1,0:T(8,128)} %probes.1, f32[128,128]{1,0:T(8,128)} %phase.1, f32[1,1,8,128,128]{4,3,2,1,0:T(8,128)} %measured.1, bf16[2,768,256]{2,1,0:T(8,128)(2,1)} %constant.4.clone.right_in, ...), custom_call_target="tpu_custom_call" | custom-call | tf_op jit(solution)/shard_map/tile_gradient/pallas_call | solution.py:537
  41.0 2.0 %settle.1 = f32[2,2,256,256]{3,2,1,0:T(8,128)} custom-call(f32[2,2,256,256]{3,2,1,0:T(8,128)} %tile_gradient.1.src), custom_call_target="tpu_custom_call" | custom-call | tf_op jit(solution)/shard_map/settle/pallas_call | solution.py:567
